TPU v7x, 32 devices: a whole 2x2x4 slice. The times are simulated.
32 devices in a mesh: groups: 2 (over y), expert: 16 (over z, x, core).
Axes of the slice: x: 2, y: 2, z: 4, core: 2. Of those that a mesh axis runs over, the one named last changes fastest.
Arguments:
- tokens: bfloat16 [4096, 2048], P(('groups', 'expert')), parts along dimension 0, may hold values from -6 to 6
- route_ids: int32 [4096, 8], P(('groups', 'expert')), parts along dimension 0, may hold values from 0 to 15, all different within a row; in each aligned block of 128 rows (0 to 127, 128 to 255, ...) at most 80 rows name the same one
- gates: float32 [4096, 8], P(('groups', 'expert')), parts along dimension 0, may hold values from 0.3 to 1
- w_gate: bfloat16 [16, 2048, 768], P('expert'), may hold values from -0.125 to 0.125
- w_up: bfloat16 [16, 2048, 768], P('expert'), may hold values from -0.125 to 0.125
- w_down: bfloat16 [16, 768, 2048], P('expert'), may hold values from -0.21875 to 0.21875
Outputs:
- combined: bfloat16 [4096, 2048], P(('groups', 'expert')), parts along dimension 0
There are 2 independent parts, one for each index of `groups`. A program takes and returns all parts, laid end to end along the dimension named above; an argument that names none is the same for every part. Nothing has to cross between parts.
Inputs may be any that keep to these rules, and one draw needn't show every extreme that they name: `route_ids`: each row names 8 different experts. In each aligned block of 128 rows (one device's tokens) no expert is named by more than 80 rows, a bound that some block reaches.
All inputs are finite; a program needn't handle non-finite values.
Results may differ from a plain program's by a relative error of at most 0.0058.
Values may be sent and summed in bfloat16 or wider, within the bound.
A program may use at most 128 MiB of HBM per device.

v0:
```python
import jax
import jax.numpy as jnp
from jax import lax
from jax.sharding import PartitionSpec as P


def expert_mlp(block_data, gate_local, up_local, down_local):
    gate_part = jnp.dot(block_data, gate_local, preferred_element_type=jnp.float32)
    up_part = jnp.dot(block_data, up_local, preferred_element_type=jnp.float32)
    hidden = (jax.nn.silu(gate_part) * up_part).astype(jnp.bfloat16)
    return jnp.dot(hidden, down_local, preferred_element_type=jnp.float32).astype(jnp.bfloat16)


def on_device(tokens, route_ids, gates, w_gate, w_up, w_down):
    n_peers = lax.axis_size("expert")
    tok_rows, top_k = route_ids.shape
    model_width = tokens.shape[1]
    capacity = 5 * tok_rows * top_k // (4 * n_peers)
    buffer_rows = n_peers * capacity
    assigned = tok_rows * top_k
    gate_local = w_gate[0]
    up_local = w_up[0]
    down_local = w_down[0]
    chosen = route_ids.reshape(-1)
    onehot = (chosen[:, None] == jnp.arange(n_peers, dtype=jnp.int32)[None, :]).astype(jnp.int32)
    running = jnp.cumsum(onehot, axis=0)
    position = jnp.sum(running * onehot, axis=1) - 1
    slot_of = chosen * capacity + position
    ordinal = jnp.arange(assigned, dtype=jnp.int32)
    anchor = jnp.zeros((buffer_rows,), jnp.int32).at[slot_of].set(ordinal)
    outgoing = tokens[anchor // top_k].reshape(n_peers, capacity, model_width)
    incoming = lax.all_to_all(outgoing, "expert", split_axis=0, concat_axis=0, tiled=True)
    n_src, n_items, _ = incoming.shape
    computed = expert_mlp(
        incoming.reshape(n_src * n_items, model_width), gate_local, up_local, down_local
    )
    computed = computed.reshape(n_src, n_items, model_width)
    returned_rows = lax.all_to_all(computed, "expert", split_axis=0, concat_axis=0, tiled=True)
    returned = returned_rows.reshape(buffer_rows, model_width)[slot_of].astype(jnp.float32)
    combined = jnp.sum(returned.reshape(tok_rows, top_k, model_width) * gates[:, :, None], axis=1)
    return combined.astype(jnp.bfloat16)


def solution(mesh):
    in_specs = (
        P(("groups", "expert"), None),
        P(("groups", "expert"), None),
        P(("groups", "expert"), None),
        P("expert", None, None),
        P("expert", None, None),
        P("expert", None, None),
    )
    out_specs = P(("groups", "expert"), None)
    return jax.shard_map(
        on_device, mesh=mesh, in_specs=in_specs, out_specs=out_specs, check_vma=False
    )
```

profile of v0, /device:TPU:15, one launch (start us, length us, event | category | flops | bytes accessed | tf_op | source)
XLA Modules:
  0.0 299.8 jit_solution(15534275883353262178)
XLA Ops:
  0.0 0.0 copy-start
  0.0 0.9 copy.11
  0.9 0.1 eq.29
  1.0 0.1 eq.25
  1.1 0.7 broadcast_multiply_fusion
  1.8 4.5 %reduce-window.6 = s32[16,8,128]{2,1,0:T(8,128)S(1)} reduce-window(s32[16,8,128]{2,1,0:T(8,128)S(1)} %fusion.8, s32[]{:T(128)} %constant.26.clone.1), window={size=1x1x128 pad=0_0x0_0x127_0}, to_apply=%region_0.0 | reduce-window | flops 2080768 | bytes 131076 | tf_op jit(solution)/shard_map/reduce-window
  6.3 0.1 slice.12
  6.4 0.1 copy.13
  6.6 0.1 copy.14
  6.7 0.1 broadcast_add_fusion
  6.8 0.1 copy.10
  6.9 0.1 mul.36
  7.0 4.3 %scatter_custom_fusion = s32[1280]{0:T(1024)S(1)} fusion(s32[1024]{0:T(1024)S(1)} %bitcast.41, s32[1024]{0:T(1024)S(1)} %iota.11, s32[]{:T(128)} %constant.26.clone.1), kind=kCustom, calls=%fused_computation.29 | custom fusion | bytes 5124 | tf_op jit(solution)/shard_map/scatter | solution.py:30
  11.4 11.9 %gather_fusion = bf16[1280,2048]{1,0:T(8,128)(2,1)} fusion(bf16[128,2048]{1,0:T(8,128)(2,1)} %param.6, s32[2048]{0:T(1024)S(1)} %pad_clamp_fusion), kind=kCustom, calls=%fused_computation | custom fusion | bytes 10490880 | tf_op jit(solution)/shard_map/gather | solution.py:31
  23.3 0.0 copy-start.2
  23.3 121.5 %all_to_all.10 = bf16[16,80,2048]{2,1,0:T(8,128)(2,1)S(1)} all-to-all(bf16[16,80,2048]{2,1,0:T(8,128)(2,1)} %bitcast.35), channel_id=1, replica_groups=mesh['groups'=2,'expert'=16] {'expert'}, dimensions={0} | all-to-all | bytes 10485760 | tf_op jit(solution)/shard_map/all_to_all | solution.py:32
  144.8 0.0 copy-done.2
  144.8 0.0 copy-start.3
  144.8 4.3 %fusion.4 = f32[1280,768]{1,0:T(8,128)S(1)} fusion(bf16[1280,2048]{1,0:T(8,128)(2,1)S(1)} %bitcast.37, bf16[1,2048,768]{2,1,0:T(8,128)(2,1)S(1)} %copy-done.2), kind=kOutput, calls=%fused_computation.10 | convolution fusion | flops 4026531840 | bytes 12320768 | tf_op jit(solution)/shard_map/dot_general | solution.py:8
  149.1 0.0 copy-done.3
  149.1 4.8 %fusion.1 = bf16[1280,768]{1,0:T(8,128)(2,1)S(1)} fusion(bf16[1280,2048]{1,0:T(8,128)(2,1)S(1)} %bitcast.38, f32[1280,768]{1,0:T(8,128)S(1)} %fusion.4, bf16[1,2048,768]{2,1,0:T(8,128)(2,1)S(1)} %copy-done.3), kind=kOutput, calls=%fused_computation.7 | convolution fusion | flops 4032430080 | bytes 14286848 | tf_op jit(solution)/shard_map/dot_general | solution.py:9
  154.0 0.0 copy-done
  154.0 6.1 %convolution_convert_fusion = bf16[1280,2048]{1,0:T(8,128)(2,1)} fusion(bf16[1280,768]{1,0:T(8,128)(2,1)S(1)} %fusion.1, bf16[1,768,2048]{2,1,0:T(8,128)(2,1)S(1)} %copy-done), kind=kOutput, calls=%fused_computation.5 | convolution fusion | flops 4029153280 | bytes 10354688 | tf_op jit(solution)/shard_map/dot_general | solution.py:11
  160.0 0.0 copy-start.1
  160.0 5.4 %all-to-all-start.1 = ((bf16[16,80,2048]{2,1,0:T(8,128)(2,1)}), bf16[16,80,2048]{2,1,0:T(8,128)(2,1)}, u32[]{:S(2)}, u32[]{:S(2)}) async-start(bf16[16,80,2048]{2,1,0:T(8,128)(2,1)} %bitcast.36), calls=%async_computation.1 | async-start | bytes 10485760 | tf_op jit(solution)/shard_map/all_to_all | solution.py:38
  165.4 0.0 copy-done.1
  165.5 0.1 copy.15
  165.6 114.8 %all-to-all-done.1 = bf16[16,80,2048]{2,1,0:T(8,128)(2,1)} async-done(((bf16[16,80,2048]{2,1,0:T(8,128)(2,1)}), bf16[16,80,2048]{2,1,0:T(8,128)(2,1)}, u32[]{:S(2)}, u32[]{:S(2)}) %all-to-all-start.1) | async-done | bytes 5242912 | tf_op jit(solution)/shard_map/all_to_all | solution.py:38
  280.4 12.0 %gather_fusion.1 = bf16[1024,2048]{1,0:T(8,128)(2,1)} fusion(bf16[1280,2048]{1,0:T(8,128)(2,1)} %bitcast.10, s32[1024]{0:T(1024)S(1)} %broadcast_clamp_fusion), kind=kCustom, calls=%fused_computation.1 | custom fusion | bytes 8392704 | tf_op jit(solution)/shard_map/gather | solution.py:39
  292.4 7.3 %fusion = bf16[128,2048]{1,0:T(8,128)(2,1)} fusion(bf16[1024,2048]{1,0:T(8,128)(2,1)} %gather_fusion.1, f32[128,8]{1,0:T(8,128)S(1)} %copy.15), kind=kLoop, calls=%fused_computation.4 | loop fusion | flops 6029312 | bytes 4722688 | tf_op jit(solution)/shard_map/reduce_sum | solution.py:40
  (10 shorter events, 0.1 us)
Async XLA Ops:
  0.0 154.0 %copy-start = (bf16[1,768,2048]{2,1,0:T(8,128)(2,1)S(1)}, bf16[1,768,2048]{2,1,0:T(8,128)(2,1)}, u32[]{:S(2)}) copy-start(bf16[1,768,2048]{2,1,0:T(8,128)(2,1)} %param.11) | copy-start | bytes 9437188
  23.3 121.5 %copy-start.2 = (bf16[1,2048,768]{2,1,0:T(8,128)(2,1)S(1)}, bf16[1,2048,768]{2,1,0:T(8,128)(2,1)}, u32[]{:S(2)}) copy-start(bf16[1,2048,768]{2,1,0:T(8,128)(2,1)} %param.9) | copy-start | bytes 9437188
  144.8 4.3 %copy-start.3 = (bf16[1,2048,768]{2,1,0:T(8,128)(2,1)S(1)}, bf16[1,2048,768]{2,1,0:T(8,128)(2,1)}, u32[]{:S(2)}) copy-start(bf16[1,2048,768]{2,1,0:T(8,128)(2,1)} %param.10) | copy-start | bytes 9437188
  160.0 5.4 %copy-start.1 = (f32[128,8]{0,1:T(8,128)S(1)}, f32[128,8]{0,1:T(8,128)}, u32[]{:S(2)}) copy-start(f32[128,8]{0,1:T(8,128)} %param.8) | copy-start | bytes 12292
  160.0 120.4 %all-to-all-start.1 = ((bf16[16,80,2048]{2,1,0:T(8,128)(2,1)}), bf16[16,80,2048]{2,1,0:T(8,128)(2,1)}, u32[]{:S(2)}, u32[]{:S(2)}) async-start(bf16[16,80,2048]{2,1,0:T(8,128)(2,1)} %bitcast.36), calls=%async_computation.1 | async-start | bytes 10485760 | tf_op jit(solution)/shard_map/all_to_all | solution.py:38
where the time goes:
time: 300 us
  blocking collectives  121 us (40%)
  waiting for transfers between devices  115 us (38%)
  local copies, waits for them, and re-layouts  30 us (10%)
  matrix products  15.2 us (5%)
  other arithmetic  12.7 us (4%)
  starting transfers between devices  5.43 us (2%)
    all_to_all x1, blocking collectives, on_device(): lax.all_to_all(outgoing, 'expert', split_axis=0, concat_axis=0, tiled=True)  121 us
    all_to_all x1, waiting for transfers between devices, on_device(): lax.all_to_all(computed, 'expert', split_axis=0, concat_axis=0, tiled=True)  115 us
    gather x1, local copies, waits for them, and re-layouts, on_device(): returned_rows.reshape(buffer_rows, model_width)[slot_of].astype(jnp.float32)  12 us
    gather x1, local copies, waits for them, and re-layouts, on_device(): outgoing = tokens[anchor // top_k].reshape(n_peers, capacity, model_width)  11.9 us
    reduce_sum x1, other arithmetic, on_device(): jnp.sum(returned.reshape(tok_rows, top_k, model_width) * gates[:, :, None...  7.32 us
    dot_general x1, matrix products, expert_mlp(): jnp.dot(hidden, down_local, preferred_element_type=jnp.float32)  6.05 us
  transfers between devices with their start and end apart: 1, of which 1 were waited for; matrix products, arithmetic and copies ran while one was open for 0% of the time, Pallas kernels for 0%

commit v1 on v0

--- a/solution.py
+++ b/solution.py
@@ -8,19 +8,31 @@
     gate_part = jnp.dot(block_data, gate_local, preferred_element_type=jnp.float32)
     up_part = jnp.dot(block_data, up_local, preferred_element_type=jnp.float32)
     hidden = (jax.nn.silu(gate_part) * up_part).astype(jnp.bfloat16)
-    return jnp.dot(hidden, down_local, preferred_element_type=jnp.float32).astype(jnp.bfloat16)
+    return jnp.dot(hidden, down_local, preferred_element_type=jnp.float32)
 
 
-def on_device(tokens, route_ids, gates, w_gate, w_up, w_down):
+def dense_on_device(tokens, route_ids, gates, w_gate, w_up, w_down):
+    n_peers = lax.axis_size("expert")
+    me = lax.axis_index("expert")
+    experts = jnp.arange(n_peers, dtype=jnp.int32)
+    weight = jnp.sum(
+        jnp.where(route_ids[:, None, :] == experts[None, :, None], gates[:, None, :], 0.0), axis=2
+    )
+    weights = lax.all_gather(weight, "expert", axis=0, tiled=True)
+    mine = lax.dynamic_slice_in_dim(weights, me, 1, axis=1)
+    everyone = lax.all_gather(tokens, "expert", axis=0, tiled=True)
+    part = expert_mlp(everyone, w_gate[0], w_up[0], w_down[0])
+    part = part.astype(jnp.bfloat16).astype(jnp.float32) * mine
+    return lax.psum_scatter(part.astype(jnp.bfloat16), "expert", scatter_dimension=0, tiled=True)
+
+
+def routed_on_device(tokens, route_ids, gates, w_gate, w_up, w_down):
     n_peers = lax.axis_size("expert")
     tok_rows, top_k = route_ids.shape
     model_width = tokens.shape[1]
     capacity = 5 * tok_rows * top_k // (4 * n_peers)
     buffer_rows = n_peers * capacity
     assigned = tok_rows * top_k
-    gate_local = w_gate[0]
-    up_local = w_up[0]
-    down_local = w_down[0]
     chosen = route_ids.reshape(-1)
     onehot = (chosen[:, None] == jnp.arange(n_peers, dtype=jnp.int32)[None, :]).astype(jnp.int32)
     running = jnp.cumsum(onehot, axis=0)
@@ -32,8 +44,8 @@
     incoming = lax.all_to_all(outgoing, "expert", split_axis=0, concat_axis=0, tiled=True)
     n_src, n_items, _ = incoming.shape
     computed = expert_mlp(
-        incoming.reshape(n_src * n_items, model_width), gate_local, up_local, down_local
-    )
+        incoming.reshape(n_src * n_items, model_width), w_gate[0], w_up[0], w_down[0]
+    ).astype(jnp.bfloat16)
     computed = computed.reshape(n_src, n_items, model_width)
     returned_rows = lax.all_to_all(computed, "expert", split_axis=0, concat_axis=0, tiled=True)
     returned = returned_rows.reshape(buffer_rows, model_width)[slot_of].astype(jnp.float32)
@@ -42,6 +54,13 @@
 
 
 def solution(mesh):
+    n_peers = mesh.shape["expert"]
+
+    def on_device(tokens, route_ids, gates, w_gate, w_up, w_down):
+        dense = n_peers <= 4 * route_ids.shape[1]
+        body = dense_on_device if dense else routed_on_device
+        return body(tokens, route_ids, gates, w_gate, w_up, w_down)
+
     in_specs = (
         P(("groups", "expert"), None),
         P(("groups", "expert"), None),

time: 300 us -> 228 us (0.76)
  the two profiles are of different devices: /device:TPU:15 before, /device:TPU:0 now
where the time goes in v1:
time: 228 us
  waiting for transfers between devices  157 us (69%)
  matrix products  32.3 us (14%)
  blocking collectives  24.1 us (11%)
  between operations  13.4 us (6%)
    reduce_scatter x1, waiting for transfers between devices, dense_on_device(): lax.psum_scatter(part.astype(jnp.bfloat16), 'expert', scatter_dimension=0...  102 us
    all_gather x1, waiting for transfers between devices, dense_on_device(): everyone = lax.all_gather(tokens, 'expert', axis=0, tiled=True)  54.4 us
    all_gather x1, blocking collectives, dense_on_device(): weights = lax.all_gather(weight, 'expert', axis=0, tiled=True)  24.1 us
    dot_general x1, matrix products, expert_mlp(): return jnp.dot(hidden, down_local, preferred_element_type=jnp.float32)  20.6 us
    dot_general x1, matrix products, expert_mlp(): jnp.dot(block_data, gate_local, preferred_element_type=jnp.float32)  11.7 us
  transfers between devices with their start and end apart: 2, of which 2 were waited for; matrix products, arithmetic and copies ran while one was open for 0% of the time, Pallas kernels for 0%

profile of v1, /device:TPU:0, one launch (start us, length us, event | category | flops | bytes accessed | tf_op | source)
XLA Modules:
  0.0 228.0 jit_solution(3535841203120528709)
XLA Ops:
  6.5 0.0 copy-start
  6.5 0.0 all-gather.2.cloned.1.call-start
  6.5 0.7 all-gather.2.cloned.1.call-update
  7.3 0.0 reduce-scatter.2.cloned.1.call-start
  7.3 0.9 select_reduce_fusion
  8.2 24.1 %all_gather.7 = f32[2048,16]{0,1:T(8,128)S(1)} all-gather(f32[128,16]{0,1:T(8,128)S(1)} %select_reduce_fusion), channel_id=1, replica_groups=mesh['groups'=2,'expert'=16] {'expert'}, dimensions={0}, use_global_device_ids=true | all-gather | bytes 139264 | tf_op jit(solution)/shard_map/all_gather | solution.py:21
  32.3 54.4 %all-gather.2.cloned.1.call-done = bf16[2048,2048]{1,0:T(8,128)(2,1)} async-done(((bf16[128,2048]{1,0:T(8,128)(2,1)}), bf16[2048,2048]{1,0:T(8,128)(2,1)}) %all-gather.2.cloned.1.call-update) | async-done | bytes 8388624 | tf_op jit(solution)/shard_map/all_gather | solution.py:23
  86.7 11.7 %fusion.3 = f32[2048,768]{1,0:T(8,128)} fusion(bf16[2048,2048]{1,0:T(8,128)(2,1)} %all-gather.2.cloned.1.call-done, bf16[1,2048,768]{2,1,0:T(8,128)(2,1)} %param.9), kind=kOutput, calls=%fused_computation.4 | convolution fusion | flops 6442450944 | bytes 17825792 | tf_op jit(solution)/shard_map/dot_general | solution.py:8
  98.4 0.0 copy-done
  98.4 20.6 %multiply_convert_fusion = bf16[2048,2048]{1,0:T(8,128)(2,1)} fusion(f32[2048]{0:T(1024)S(1)} %bitcast.13, f32[2048,768]{1,0:T(8,128)} %fusion.3, bf16[2048,2048]{1,0:T(8,128)(2,1)} %all-gather.2.cloned.1.call-done, bf16[1,768,2048]{2,1,0:T(8,128)(2,1)S(1)} %copy-done, bf16[1,2048,768]{2,1,0:T(8,128)(2,1)} %param.10), kind=kOutput, calls=%fused_computation | convolution fusion | flops 12911116288 | bytes 29368320 | tf_op jit(solution)/shard_map/dot_general | solution.py:11
  119.0 0.0 reduce-scatter.2.cloned.1.call-update
  119.0 102.2 %reduce-scatter.2.cloned.1.call-done = bf16[128,2048]{1,0:T(8,128)(2,1)} async-done(((bf16[2048,2048]{1,0:T(8,128)(2,1)}), bf16[128,2048]{1,0:T(8,128)(2,1)}) %reduce-scatter.2.cloned.1.call-update) | async-done | bytes 524304 | tf_op jit(solution)/shard_map/reduce_scatter | solution.py:26
  (1 shorter events, 0.0 us)
Async XLA Ops:
  6.5 91.9 %copy-start = (bf16[1,768,2048]{2,1,0:T(8,128)(2,1)S(1)}, bf16[1,768,2048]{2,1,0:T(8,128)(2,1)}, u32[]{:S(2)}) copy-start(bf16[1,768,2048]{2,1,0:T(8,128)(2,1)} %param.11) | copy-start | bytes 9437188
  6.5 80.2 %all-gather.2.cloned.1.call-start = ((), (), s32[]{:S(2)}) async-start(), calls=%async_computation.1 | async-start | bytes 8912896 | tf_op jit(solution)/shard_map/all_gather | solution.py:23
  7.3 213.9 %reduce-scatter.2.cloned.1.call-start = ((), (), s32[]{:S(2)}) async-start(), calls=%async_computation.2 | async-start | bytes 8912896 | tf_op jit(solution)/shard_map/reduce_scatter | solution.py:26
Sparse Core Ops, SparseCore 0:
  9.5 77.1 all-gather.1
  119.1 102.0 reduce-scatter.1

commit v2 on v1

--- a/solution.py
+++ b/solution.py
@@ -1,6 +1,10 @@
+import functools
+
 import jax
 import jax.numpy as jnp
 from jax import lax
+from jax.experimental import pallas as pl
+from jax.experimental.pallas import tpu as pltpu
 from jax.sharding import PartitionSpec as P
 
 
@@ -11,19 +15,317 @@
     return jnp.dot(hidden, down_local, preferred_element_type=jnp.float32)
 
 
+MESH = pl.DeviceIdType.MESH
+
+
+def layer_kernel(
+    n, rows, tok_ref, weight_ref, wg_hbm, wu_hbm, wd_hbm, out_ref,
+    wg, wu, wd, held, gain, own, to_mate, from_mate, to_side, from_side, to_line, from_line,
+    load_sem, gain_send, gain_recv, tok_recv, up_send, down_send, side_send, mate_send,
+    mate_part_send, mate_part_recv, side_part_send, side_part_recv, line_part_send, line_part_recv,
+):
+    length = n // 4
+    me = lax.axis_index("expert")
+    c = lax.rem(me, 2)
+    x = lax.rem(me // 2, 2)
+    z = me // 4
+
+    def index(z_at, x_at, c_at):
+        return (z_at * 2 + x_at) * 2 + c_at
+
+    mate = index(z, x, 1 - c)
+    side = index(z, 1 - x, c)
+    above = index(lax.rem(z + 1, length), x, c)
+    below = index(lax.rem(z + length - 1, length), x, c)
+    has_above = z < length - 1
+    has_below = z > 0
+
+    def block(ref, at):
+        return ref.at[pl.ds(pl.multiple_of(at * rows, rows), rows), :]
+
+    def remote(src, dst, send, recv, to):
+        return pltpu.make_async_remote_copy(
+            src_ref=src, dst_ref=dst, send_sem=send, recv_sem=recv,
+            device_id={"expert": to}, device_id_type=MESH,
+        )
+
+    def nearest(k):
+        both = jnp.minimum(z, length - 1 - z)
+        near = (k + 1) // 2
+        near = jnp.where(lax.rem(k, 2) == 1, near, -near)
+        far = jnp.where(2 * z < length - 1, k - both, both - k)
+        return z + jnp.where(k <= 2 * both, near, far)
+
+    loads = [
+        pltpu.make_async_copy(tok_ref, block(held, me), load_sem.at[0]),
+        pltpu.make_async_copy(weight_ref.at[me], gain.at[me], load_sem.at[1]),
+        pltpu.make_async_copy(wg_hbm, wg, load_sem.at[2]),
+        pltpu.make_async_copy(wu_hbm, wu, load_sem.at[3]),
+        pltpu.make_async_copy(wd_hbm, wd, load_sem.at[4]),
+    ]
+    for load in loads:
+        load.start()
+
+    barrier = pltpu.get_barrier_semaphore()
+    for step in range(1, n):
+        pl.semaphore_signal(
+            barrier, inc=1, device_id={"expert": lax.rem(me + step, n)}, device_id_type=MESH
+        )
+    pl.semaphore_wait(barrier, n - 1)
+
+    def tok_up(at):
+        s = index(at, x, c)
+        return remote(block(held, s), block(held, s), up_send.at[at], tok_recv.at[s], above)
+
+    def tok_down(at):
+        s = index(at, x, c)
+        return remote(block(held, s), block(held, s), down_send.at[at], tok_recv.at[s], below)
+
+    def tok_side(at):
+        s = index(at, x, c)
+        return remote(block(held, s), block(held, s), side_send.at[at], tok_recv.at[s], side)
+
+    def tok_mate(s):
+        return remote(block(held, s), block(held, s), mate_send.at[s // 2], tok_recv.at[s], mate)
+
+    def tok_wait(s):
+        remote(block(held, s), block(held, s), mate_send.at[0], tok_recv.at[s], mate).wait_recv()
+
+    def gain_copy(to):
+        return remote(weight_ref.at[to], gain.at[me], gain_send.at[to], gain_recv.at[me], to)
+
+    loads[0].wait()
+    tok_mate(me).start()
+
+    @pl.when(has_above)
+    def _():
+        tok_up(z).start()
+
+    @pl.when(has_below)
+    def _():
+        tok_down(z).start()
+
+    tok_side(z).start()
+    for step in range(1, n):
+        gain_copy(lax.rem(me + step, n)).start()
+    for load in loads[1:]:
+        load.wait()
+
+    def mate_part(at):
+        return remote(
+            block(to_mate, at), block(from_mate, at), mate_part_send.at[at], mate_part_recv.at[at], mate
+        )
+
+    def side_part(at):
+        return remote(
+            block(to_side, at), block(from_side, at), side_part_send.at[at], side_part_recv.at[at], side
+        )
+
+    def column(at):
+        return jnp.transpose(gain[at])[:, 0:1]
+
+    def expert(z_at, x_at):
+        node = z_at * 2 + x_at
+        mine, other = node * 2 + c, node * 2 + 1 - c
+        for at in (mine, other):
+            @pl.when(at != me)
+            def _():
+                remote(weight_ref.at[0], gain.at[at], gain_send.at[0], gain_recv.at[at], mate).wait_recv()
+        data = jnp.concatenate([block(held, mine)[...], block(held, other)[...]], axis=0)
+        gate_part = jnp.dot(data, wg[...], preferred_element_type=jnp.float32)
+        up_part = jnp.dot(data, wu[...], preferred_element_type=jnp.float32)
+        hidden = (gate_part / (1.0 + jnp.exp(-gate_part)) * up_part).astype(jnp.bfloat16)
+        own_gain, other_gain = column(mine), column(other)
+        width = wd.shape[1] // 4
+        for piece in range(4):
+            cols = slice(piece * width, (piece + 1) * width)
+            out = jnp.dot(hidden, wd[:, cols], preferred_element_type=jnp.float32)
+            out = out.astype(jnp.bfloat16).astype(jnp.float32)
+            block(own, node)[:, cols] = out[:rows] * own_gain
+            block(to_mate, node)[:, cols] = (out[rows:] * other_gain).astype(jnp.bfloat16)
+        mate_part(node).start()
+
+    def across(z_at):
+        node = z_at * 2 + 1 - x
+        mate_part(node).wait_recv()
+        block(to_side, z_at)[...] = (
+            block(own, node)[...] + block(from_mate, node)[...].astype(jnp.float32)
+        ).astype(jnp.bfloat16)
+        side_part(z_at).start()
+
+    def step(t, carry):
+        odd = lax.rem(t, 2)
+        k = (t + 1) // 2
+
+        @pl.when((odd == 1) & (k < length))
+        def _():
+            at = nearest(k)
+            s = index(at, x, c)
+            tok_wait(s)
+
+            @pl.when((at < z) & has_above)
+            def _():
+                tok_up(at).start()
+
+            @pl.when((at > z) & has_below)
+            def _():
+                tok_down(at).start()
+
+            tok_side(at).start()
+            tok_mate(s).start()
+
+        x_at = lax.rem(x + odd, 2)
+        z_at = nearest(k - odd)
+
+        @pl.when(odd == 1)
+        def _():
+            s = index(z_at, 1 - x, c)
+            tok_wait(s)
+            tok_mate(s).start()
+
+        tok_wait(index(z_at, x_at, 1 - c))
+        expert(z_at, x_at)
+
+        @pl.when((odd == 0) & (t > 0))
+        def _():
+            across(nearest(k - 1))
+
+        return carry
+
+    lax.fori_loop(0, 2 * length, step, 0)
+    across(nearest(length - 1))
+
+    def gathered(z_at):
+        node = z_at * 2 + x
+        mate_part(node).wait_recv()
+        side_part(z_at).wait_recv()
+        return (
+            block(own, node)[...]
+            + block(from_mate, node)[...].astype(jnp.float32)
+            + block(from_side, z_at)[...].astype(jnp.float32)
+        )
+
+    def line_wait(slot):
+        remote(
+            block(to_line, 0), block(from_line, slot), line_part_send.at[0], line_part_recv.at[slot], mate
+        ).wait_recv()
+
+    def line_part(z_at, slot, to):
+        return remote(
+            block(to_line, z_at), block(from_line, slot), line_part_send.at[z_at], line_part_recv.at[slot], to
+        )
+
+    def relay(j, carry):
+        low = length - 1 - z
+        up_first = jnp.where(j < low, z + 1 + j, z - 1 - (j - low))
+        down_first = jnp.where(j < z, z - 1 - j, z + 1 + (j - z))
+        z_at = jnp.where(2 * z < length, up_first, down_first)
+        is_up = z_at > z
+        behind = (is_up & has_below) | ((z_at < z) & has_above)
+
+        @pl.when(behind)
+        def _():
+            total = gathered(z_at)
+            line_wait(z_at)
+            block(to_line, z_at)[...] = (
+                total + block(from_line, z_at)[...].astype(jnp.float32)
+            ).astype(jnp.bfloat16)
+
+        @pl.when(jnp.logical_not(behind))
+        def _():
+            block(to_line, z_at)[...] = gathered(z_at).astype(jnp.bfloat16)
+
+        @pl.when(is_up)
+        def _():
+            line_part(z_at, z_at, above).start()
+
+        @pl.when(z_at < z)
+        def _():
+            line_part(z_at, jnp.where(z_at == z - 1, length, z_at), below).start()
+
+        return carry
+
+    lax.fori_loop(0, length - 1, relay, 0)
+    block(own, z * 2 + x)[...] = gathered(z)
+
+    @pl.when(has_below)
+    def _():
+        line_wait(z)
+        block(own, z * 2 + x)[...] += block(from_line, z)[...].astype(jnp.float32)
+
+    @pl.when(has_above)
+    def _():
+        line_wait(length)
+        block(own, z * 2 + x)[...] += block(from_line, length)[...].astype(jnp.float32)
+
+    out_ref[...] = block(own, z * 2 + x)[...].astype(out_ref.dtype)
+
+    def drain(at, carry):
+        @pl.when((at <= z) & has_above)
+        def _():
+            tok_up(at).wait_send()
+
+        @pl.when((at >= z) & has_below)
+        def _():
+            tok_down(at).wait_send()
+
+        tok_side(at).wait_send()
+        for x_at in range(2):
+            tok_mate(index(at, x_at, c)).wait_send()
+            mate_part(at * 2 + x_at).wait_send()
+        side_part(at).wait_send()
+
+        @pl.when(at != z)
+        def _():
+            line_part(at, at, mate).wait_send()
+
+        return carry
+
+    lax.fori_loop(0, length, drain, 0)
+    for step_at in range(1, n):
+        gain_copy(lax.rem(me + step_at, n)).wait_send()
+
+
 def dense_on_device(tokens, route_ids, gates, w_gate, w_up, w_down):
-    n_peers = lax.axis_size("expert")
-    me = lax.axis_index("expert")
-    experts = jnp.arange(n_peers, dtype=jnp.int32)
+    n = lax.axis_size("expert")
+    rows, width = tokens.shape
+    experts = jnp.arange(n, dtype=jnp.int32)
     weight = jnp.sum(
-        jnp.where(route_ids[:, None, :] == experts[None, :, None], gates[:, None, :], 0.0), axis=2
+        jnp.where(route_ids.T[None, :, :] == experts[:, None, None], gates.T[None, :, :], 0.0), axis=1
     )
-    weights = lax.all_gather(weight, "expert", axis=0, tiled=True)
-    mine = lax.dynamic_slice_in_dim(weights, me, 1, axis=1)
-    everyone = lax.all_gather(tokens, "expert", axis=0, tiled=True)
-    part = expert_mlp(everyone, w_gate[0], w_up[0], w_down[0])
-    part = part.astype(jnp.bfloat16).astype(jnp.float32) * mine
-    return lax.psum_scatter(part.astype(jnp.bfloat16), "expert", scatter_dimension=0, tiled=True)
+    weight = jnp.broadcast_to(weight[:, None, :], (n, 8, rows))
+    nodes, length = n // 2, n // 4
+    bf16, f32 = jnp.bfloat16, jnp.float32
+    dma = pltpu.SemaphoreType.DMA
+    vmem = pltpu.VMEM
+    any_spec = pl.BlockSpec(memory_space=pl.ANY)
+    vmem_spec = pl.BlockSpec(memory_space=pltpu.VMEM)
+    return pl.pallas_call(
+        functools.partial(layer_kernel, n, rows),
+        out_shape=jax.ShapeDtypeStruct((rows, width), bf16),
+        in_specs=[any_spec, vmem_spec, any_spec, any_spec, any_spec],
+        out_specs=vmem_spec,
+        scratch_shapes=[
+            vmem(w_gate.shape[1:], bf16),
+            vmem(w_up.shape[1:], bf16),
+            vmem(w_down.shape[1:], bf16),
+            vmem((n * rows, width), bf16),
+            vmem((n, 8, rows), f32),
+            vmem((nodes * rows, width), f32),
+            vmem((nodes * rows, width), bf16),
+            vmem((nodes * rows, width), bf16),
+            vmem((length * rows, width), bf16),
+            vmem((length * rows, width), bf16),
+            vmem((length * rows, width), bf16),
+            vmem(((length + 1) * rows, width), bf16),
+            dma((5,)), dma((n,)), dma((n,)), dma((n,)),
+            dma((length,)), dma((length,)), dma((length,)), dma((nodes,)),
+            dma((nodes,)), dma((nodes,)), dma((length,)), dma((length,)), dma((length,)), dma((length + 1,)),
+        ],
+        compiler_params=pltpu.CompilerParams(
+            collective_id=0, has_side_effects=True, vmem_limit_bytes=60 * 1024 * 1024
+        ),
+    )(tokens, weight, w_gate[0], w_up[0], w_down[0])
 
 
 def routed_on_device(tokens, route_ids, gates, w_gate, w_up, w_down):

time: 228 us -> 145 us (0.64)
  waiting for transfers between devices: 157 us -> 0 us
  Pallas kernels: 0 us -> 142 us
  matrix products: 32.3 us -> 0 us
  blocking collectives: 24.1 us -> 0 us
  between operations: 13.4 us -> 0.01 us
    pallas_call x0 -> x1, Pallas kernels: none -> 142 us  [dense_on_device(): pl.pallas_call(functools.partial(layer_kernel, n, rows), out_shape=jax.Sh...]
    reduce_scatter x1 -> x0, waiting for transfers between devices: 102 us -> none  [dense_on_device(): lax.psum_scatter(part.astype(jnp.bfloat16), 'expert', scatter_dimension=0...]
    all_gather x1 -> x0, waiting for transfers between devices: 54.4 us -> none  [dense_on_device(): everyone = lax.all_gather(tokens, 'expert', axis=0, tiled=True)]
    dot_general x2 -> x0, matrix products: 32.3 us -> none  [the longest x1 20.6 us: expert_mlp(): return jnp.dot(hidden, down_local, preferred_element_type=jnp.float32)]
    all_gather x1 -> x0, blocking collectives: 24.1 us -> none  [dense_on_device(): weights = lax.all_gather(weight, 'expert', axis=0, tiled=True)]
  transfers between devices with their start and end apart: 2 -> 0, of which waited for: 2 -> 0; matrix products, arithmetic and copies ran while one was open for 0% -> 0% of each run, Pallas kernels for 0% -> 0%
where the time goes in v2:
time: 145 us
  Pallas kernels  142 us (98%)
  local copies, waits for them, and re-layouts  1.88 us (1%)
    pallas_call x1, Pallas kernels, dense_on_device(): pl.pallas_call(functools.partial(layer_kernel, n, rows), out_shape=jax.Sh...  142 us

profile of v2, /device:TPU:0, one launch (start us, length us, event | category | flops | bytes accessed | tf_op | source)
XLA Modules:
  0.0 145.3 jit_solution(15518184455583417081)
XLA Ops:
  0.0 1.4 fusion.weight_ref
  1.4 142.0 %shard_map.64 = bf16[128,2048]{1,0:T(8,128)(2,1)} custom-call(bf16[128,2048]{1,0:T(8,128)(2,1)} %tok_ref.1, f32[16,8,128]{2,1,0:T(8,128)} %fusion.weight_ref, bf16[2048,768]{1,0:T(8,128)(2,1)} %bitcast.5, bf16[2048,768]{1,0:T(8,128)(2,1)} %bitcast.6, bf16[768,2048]{1,0:T(8,128)(2,1)} %bitcast.7), custom_call_target="tpu_custom_call" | custom-call | tf_op jit(solution)/shard_map/pallas_call | solution.py:303
  143.4 1.9 %copy.8 = bf16[128,2048]{1,0:T(8,128)(2,1)} copy(bf16[128,2048]{1,0:T(8,128)(2,1)} %shard_map.64) | data formatting | bytes 1048576

commit v3 on v1

--- a/solution.py
+++ b/solution.py
@@ -1,6 +1,10 @@
+import functools
+
 import jax
 import jax.numpy as jnp
 from jax import lax
+from jax.experimental import pallas as pl
+from jax.experimental.pallas import tpu as pltpu
 from jax.sharding import PartitionSpec as P
 
 
@@ -11,19 +15,386 @@
     return jnp.dot(hidden, down_local, preferred_element_type=jnp.float32)
 
 
+MESH = pl.DeviceIdType.MESH
+
+
+def layer_kernel(
+    n, rows, parts, group, crossing, late, tok_ref, weight_ref, wg_hbm, wu_hbm, wd_hbm, out_ref,
+    wg, wu, wd, held, gain, spread, own, to_mate, from_mate, to_side, from_side, to_line, from_line,
+    load_sem, gain_send, gain_recv, tok_recv, up_send, down_send, side_send, mate_send,
+    mate_part_send, mate_part_recv, side_part_send, side_part_recv, line_part_send, line_part_recv,
+):
+    length = n // 4
+    me = lax.axis_index("expert")
+    c = lax.rem(me, 2)
+    x = lax.rem(me // 2, 2)
+    z = me // 4
+
+    def index(z_at, x_at, c_at):
+        return (z_at * 2 + x_at) * 2 + c_at
+
+    mate = index(z, x, 1 - c)
+    side = index(z, 1 - x, c)
+    above = index(lax.rem(z + 1, length), x, c)
+    below = index(lax.rem(z + length - 1, length), x, c)
+    has_above = z < length - 1
+    has_below = z > 0
+
+    count = rows // parts
+
+    def block(ref, at):
+        return ref.at[pl.ds(pl.multiple_of(at * rows, rows), rows), :]
+
+    def piece(ref, at, p):
+        return ref.at[pl.ds(pl.multiple_of(at * rows + p * count, count), count), :]
+
+    def one_of(p, chosen):
+        found = p < 0
+        for q in chosen:
+            found = found | (p == q)
+        return found
+
+    def remote(src, dst, send, recv, to):
+        return pltpu.make_async_remote_copy(
+            src_ref=src, dst_ref=dst, send_sem=send, recv_sem=recv,
+            device_id={"expert": to}, device_id_type=MESH,
+        )
+
+    def nearest(k):
+        both = jnp.minimum(z, length - 1 - z)
+        near = (k + 1) // 2
+        near = jnp.where(lax.rem(k, 2) == 1, near, -near)
+        far = jnp.where(2 * z < length - 1, k - both, both - k)
+        return z + jnp.where(k <= 2 * both, near, far)
+
+    loads = [
+        pltpu.make_async_copy(tok_ref, block(held, me), load_sem.at[0]),
+        pltpu.make_async_copy(weight_ref.at[me], gain.at[me], load_sem.at[1]),
+        pltpu.make_async_copy(wg_hbm, wg, load_sem.at[2]),
+        pltpu.make_async_copy(wu_hbm, wu, load_sem.at[3]),
+        pltpu.make_async_copy(wd_hbm, wd, load_sem.at[4]),
+    ]
+    for load in loads:
+        load.start()
+
+    barrier = pltpu.get_barrier_semaphore()
+    for step in range(1, n):
+        pl.semaphore_signal(
+            barrier, inc=1, device_id={"expert": lax.rem(me + step, n)}, device_id_type=MESH
+        )
+    pl.semaphore_wait(barrier, n - 1)
+
+    def tok(p, s, sends, slot, to):
+        return remote(piece(held, s, p), piece(held, s, p), sends.at[p, slot], tok_recv.at[p, s], to)
+
+    def tok_up(p, s):
+        return tok(p, s, up_send, s // 2, above)
+
+    def tok_down(p, s):
+        return tok(p, s, down_send, s // 2, below)
+
+    def tok_side(p, s):
+        return tok(p, s, side_send, s // 4, side)
+
+    def tok_mate(p, s):
+        return tok(p, s, mate_send, s // 2, mate)
+
+    def tok_wait(p, s):
+        tok_mate(p, s).wait_recv()
+
+    def pass_on(p, s, at):
+        @pl.when((at <= z) & has_above)
+        def _():
+            tok_up(p, s).start()
+
+        @pl.when((at >= z) & has_below)
+        def _():
+            tok_down(p, s).start()
+
+    def gain_copy(to):
+        return remote(weight_ref.at[to], gain.at[me], gain_send.at[to], gain_recv.at[me], to)
+
+    def mate_part(p, node):
+        return remote(
+            piece(to_mate, node, p), piece(from_mate, node, p),
+            mate_part_send.at[p, node], mate_part_recv.at[p, node], mate,
+        )
+
+    def side_part(p, at):
+        return remote(
+            piece(to_side, at, p), piece(from_side, at, p),
+            side_part_send.at[p, at], side_part_recv.at[p, at], side,
+        )
+
+    def line_part(p, node, slot, to):
+        return remote(
+            piece(to_line, node, p), piece(from_line, slot, p),
+            line_part_send.at[p, node], line_part_recv.at[p, slot], to,
+        )
+
+    def own_column(p, k):
+        at = nearest(k)
+        s = index(at, x, c)
+
+        @pl.when(k > 0)
+        def _():
+            tok_wait(p, s)
+
+        pass_on(p, s, at)
+
+        @pl.when((k == 0) | jnp.logical_not(one_of(p, crossing)))
+        def _():
+            tok_side(p, s).start()
+
+        tok_mate(p, s).start()
+
+    def other_column(p, k):
+        at = nearest(k)
+        s = index(at, 1 - x, c)
+        tok_wait(p, s)
+
+        @pl.when(one_of(p, crossing))
+        def _():
+            pass_on(p, s, at)
+
+        tok_mate(p, s).start()
+
+    def expert(p, k):
+        @pl.when(lax.rem(k, group) == group - 1)
+        def _():
+            run_expert(p, [nearest(k - back) for back in reversed(range(group))])
+
+    def run_expert(p, places):
+        mine = [index(z_at, x_at, c) for z_at in places for x_at in (x, 1 - x)]
+        others = [index(z_at, x_at, 1 - c) for z_at in places for x_at in (x, 1 - x)]
+        for s in others:
+            tok_wait(p, s)
+
+        @pl.when(p == 0)
+        def _():
+            for s in mine + others:
+                @pl.when(s != me)
+                def _():
+                    remote(weight_ref.at[0], gain.at[s], gain_send.at[0], gain_recv.at[s], mate).wait_recv()
+
+                block(spread, s)[...] = jnp.broadcast_to(jnp.transpose(gain[s])[:, 0:1], (rows, 128))
+
+        data = jnp.concatenate([piece(held, s, p)[...] for s in mine + others], axis=0)
+        gate_part = jnp.dot(data, wg[...], preferred_element_type=jnp.float32)
+        up_part = jnp.dot(data, wu[...], preferred_element_type=jnp.float32)
+        hidden = (gate_part / (1.0 + jnp.exp(-gate_part)) * up_part).astype(jnp.bfloat16)
+        scale = jnp.concatenate([piece(spread, s, p)[:, 0:1] for s in mine + others], axis=0)
+        width = wd.shape[1] // 4
+        for column in range(4):
+            cols = slice(column * width, (column + 1) * width)
+            out = jnp.dot(hidden, wd[:, cols], preferred_element_type=jnp.float32)
+            out = out.astype(jnp.bfloat16).astype(jnp.float32) * scale
+            for place, s in enumerate(mine):
+                piece(own, s // 2, p)[:, cols] = out[place * count:(place + 1) * count]
+            for place, s in enumerate(others):
+                piece(to_mate, s // 2, p)[:, cols] = out[(len(mine) + place) * count:(len(mine) + place + 1) * count].astype(jnp.bfloat16)
+        for s in others[::-1]:
+            mate_part(p, s // 2).start()
+
+    def across(p, k):
+        z_at = nearest(k)
+        for x_at in (1 - x, x):
+            node = z_at * 2 + x_at
+            mate_part(p, node).wait_recv()
+            piece(own, node, p)[...] += piece(from_mate, node, p)[...].astype(jnp.float32)
+
+        @pl.when(jnp.logical_not(one_of(p, late)))
+        def _():
+            piece(to_side, z_at, p)[...] = piece(own, z_at * 2 + 1 - x, p)[...].astype(jnp.bfloat16)
+            side_part(p, z_at).start()
+
+    def add_line(p, node, slot):
+        line_part(p, 0, slot, mate).wait_recv()
+        piece(own, node, p)[...] += piece(from_line, slot, p)[...].astype(jnp.float32)
+
+    def add_side(p, z_at):
+        side_part(p, z_at).wait_recv()
+        piece(own, z_at * 2 + x, p)[...] += piece(from_side, z_at, p)[...].astype(jnp.float32)
+
+    def relay_one(p, z_at, x_at, behind, slot, to):
+        node = z_at * 2 + x_at
+
+        @pl.when(behind)
+        def _():
+            add_line(p, node, node)
+
+        piece(to_line, node, p)[...] = piece(own, node, p)[...].astype(jnp.bfloat16)
+        line_part(p, node, slot, to).start()
+
+    def relay_both(p, z_at, behind, step_to, to):
+        def slot(x_at):
+            landing = jnp.where((step_to < 0) & (z_at == z - 1), length, z_at)
+            return landing * 2 + x_at
+
+        @pl.when(one_of(p, late))
+        def _():
+            relay_one(p, z_at, 1 - x, behind, slot(1 - x), to)
+
+        @pl.when(jnp.logical_not(one_of(p, late)))
+        def _():
+            add_side(p, z_at)
+
+        relay_one(p, z_at, x, behind, slot(x), to)
+
+    def relay(p, moment):
+        up_at = moment - z
+        down_at = 2 * length - 2 - z - moment
+
+        @pl.when((up_at > z) & (up_at < length))
+        def _():
+            relay_both(p, up_at, has_below, 1, above)
+
+        @pl.when((down_at < z) & (down_at >= 0))
+        def _():
+            relay_both(p, down_at, has_above, -1, below)
+
+    def collect(p, x_at):
+        @pl.when(has_below)
+        def _():
+            add_line(p, z * 2 + x_at, z * 2 + x_at)
+
+        @pl.when(has_above)
+        def _():
+            add_line(p, z * 2 + x_at, length * 2 + x_at)
+
+    def finish(p):
+        @pl.when(one_of(p, late))
+        def _():
+            collect(p, 1 - x)
+            piece(to_side, z, p)[...] = piece(own, z * 2 + 1 - x, p)[...].astype(jnp.bfloat16)
+            side_part(p, z).start()
+
+        collect(p, x)
+        add_side(p, z)
+        piece(out_ref, 0, p)[...] = piece(own, z * 2 + x, p)[...].astype(out_ref.dtype)
+
+    def at_step(i, body):
+        @pl.when((i >= 0) & (i < parts * length))
+        def _():
+            body(i // length, lax.rem(i, length))
+
+    def returned(p, k):
+        relay(p, k + 1)
+
+    def returned_far(p, k):
+        relay(p, k + 1 + length)
+
+        @pl.when(k == length - 2)
+        def _():
+            finish(p)
+
+    loads[0].wait()
+    own_column(0, 0)
+    for step in range(1, n):
+        gain_copy(lax.rem(me + step, n)).start()
+    for load in loads[1:]:
+        load.wait()
+
+    def step(i, carry):
+        @pl.when(i > 0)
+        def _():
+            at_step(i, own_column)
+
+        at_step(i - OTHER_LAG, other_column)
+        at_step(i - EXPERT_LAG, expert)
+        at_step(i - ACROSS_LAG, across)
+        at_step(i - RETURN_LAG - length, returned_far)
+        at_step(i - RETURN_LAG, returned)
+        return carry
+
+    lax.fori_loop(0, (parts + 1) * length + RETURN_LAG - 1, step, 0)
+
+    def drain(i, carry):
+        p, at = i // length, lax.rem(i, length)
+        crosses, is_late = one_of(p, crossing), one_of(p, late)
+        for x_at in range(2):
+            s = index(at, x_at, c)
+            here = x_at == x
+            tok_mate(p, s).wait_send()
+
+            @pl.when((at <= z) & has_above & (crosses | here))
+            def _():
+                tok_up(p, s).wait_send()
+
+            @pl.when((at >= z) & has_below & (crosses | here))
+            def _():
+                tok_down(p, s).wait_send()
+
+            mate_part(p, at * 2 + x_at).wait_send()
+
+            @pl.when((at != z) & (is_late | here))
+            def _():
+                line_part(p, at * 2 + x_at, 0, mate).wait_send()
+
+        @pl.when((at == z) | jnp.logical_not(crosses))
+        def _():
+            tok_side(p, index(at, x, c)).wait_send()
+
+        @pl.when((at == z) | jnp.logical_not(is_late))
+        def _():
+            side_part(p, at).wait_send()
+
+        return carry
+
+    lax.fori_loop(0, parts * length, drain, 0)
+    for step_at in range(1, n):
+        gain_copy(lax.rem(me + step_at, n)).wait_send()
+
+
+PARTS = 4
+GROUP = 1
+CROSSING = ()
+LATE = ()
+OTHER_LAG, EXPERT_LAG, ACROSS_LAG, RETURN_LAG = 1, 2, 3, 5
+
+
 def dense_on_device(tokens, route_ids, gates, w_gate, w_up, w_down):
-    n_peers = lax.axis_size("expert")
-    me = lax.axis_index("expert")
-    experts = jnp.arange(n_peers, dtype=jnp.int32)
+    n = lax.axis_size("expert")
+    rows, width = tokens.shape
+    experts = jnp.arange(n, dtype=jnp.int32)
     weight = jnp.sum(
-        jnp.where(route_ids[:, None, :] == experts[None, :, None], gates[:, None, :], 0.0), axis=2
+        jnp.where(route_ids.T[None, :, :] == experts[:, None, None], gates.T[None, :, :], 0.0), axis=1
     )
-    weights = lax.all_gather(weight, "expert", axis=0, tiled=True)
-    mine = lax.dynamic_slice_in_dim(weights, me, 1, axis=1)
-    everyone = lax.all_gather(tokens, "expert", axis=0, tiled=True)
-    part = expert_mlp(everyone, w_gate[0], w_up[0], w_down[0])
-    part = part.astype(jnp.bfloat16).astype(jnp.float32) * mine
-    return lax.psum_scatter(part.astype(jnp.bfloat16), "expert", scatter_dimension=0, tiled=True)
+    weight = jnp.broadcast_to(weight[:, None, :], (n, 8, rows))
+    nodes, length = n // 2, n // 4
+    bf16, f32 = jnp.bfloat16, jnp.float32
+    dma = pltpu.SemaphoreType.DMA
+    vmem = pltpu.VMEM
+    any_spec = pl.BlockSpec(memory_space=pl.ANY)
+    vmem_spec = pl.BlockSpec(memory_space=pltpu.VMEM)
+    return pl.pallas_call(
+        functools.partial(layer_kernel, n, rows, PARTS, GROUP, CROSSING, LATE),
+        out_shape=jax.ShapeDtypeStruct((rows, width), bf16),
+        in_specs=[any_spec, vmem_spec, any_spec, any_spec, any_spec],
+        out_specs=vmem_spec,
+        scratch_shapes=[
+            vmem(w_gate.shape[1:], bf16),
+            vmem(w_up.shape[1:], bf16),
+            vmem(w_down.shape[1:], bf16),
+            vmem((n * rows, width), bf16),
+            vmem((n, 8, rows), f32),
+            vmem((n * rows, 128), f32),
+            vmem((nodes * rows, width), f32),
+            vmem((nodes * rows, width), bf16),
+            vmem((nodes * rows, width), bf16),
+            vmem((length * rows, width), bf16),
+            vmem((length * rows, width), bf16),
+            vmem((nodes * rows, width), bf16),
+            vmem(((nodes + 2) * rows, width), bf16),
+            dma((5,)), dma((n,)), dma((n,)), dma((PARTS, n)),
+            dma((PARTS, nodes)), dma((PARTS, nodes)), dma((PARTS, length)), dma((PARTS, nodes)),
+            dma((PARTS, nodes)), dma((PARTS, nodes)), dma((PARTS, length)), dma((PARTS, length)),
+            dma((PARTS, nodes)), dma((PARTS, nodes + 2)),
+        ],
+        compiler_params=pltpu.CompilerParams(
+            collective_id=0, has_side_effects=True, vmem_limit_bytes=60 * 1024 * 1024
+        ),
+    )(tokens, weight, w_gate[0], w_up[0], w_down[0])
 
 
 def routed_on_device(tokens, route_ids, gates, w_gate, w_up, w_down):

time: 228 us -> 127 us (0.56)
  waiting for transfers between devices: 157 us -> 0 us
  Pallas kernels: 0 us -> 123 us
  matrix products: 32.3 us -> 0 us
  blocking collectives: 24.1 us -> 0 us
  between operations: 13.4 us -> 0.01 us
    pallas_call x0 -> x1, Pallas kernels: none -> 123 us  [dense_on_device(): pl.pallas_call(functools.partial(layer_kernel, n, rows, PARTS, GROUP, CRO...]
    reduce_scatter x1 -> x0, waiting for transfers between devices: 102 us -> none  [dense_on_device(): lax.psum_scatter(part.astype(jnp.bfloat16), 'expert', scatter_dimension=0...]
    all_gather x1 -> x0, waiting for transfers between devices: 54.4 us -> none  [dense_on_device(): everyone = lax.all_gather(tokens, 'expert', axis=0, tiled=True)]
    dot_general x2 -> x0, matrix products: 32.3 us -> none  [the longest x1 20.6 us: expert_mlp(): return jnp.dot(hidden, down_local, preferred_element_type=jnp.float32)]
    all_gather x1 -> x0, blocking collectives: 24.1 us -> none  [dense_on_device(): weights = lax.all_gather(weight, 'expert', axis=0, tiled=True)]
  transfers between devices with their start and end apart: 2 -> 0, of which waited for: 2 -> 0; matrix products, arithmetic and copies ran while one was open for 0% -> 0% of each run, Pallas kernels for 0% -> 0%
where the time goes in v3:
time: 127 us; the launch traced here: 126 us
  Pallas kernels  123 us (97%)
  local copies, waits for them, and re-layouts  1.88 us (1%)
  other arithmetic  1.35 us (1%)
    pallas_call x1, Pallas kernels, dense_on_device(): pl.pallas_call(functools.partial(layer_kernel, n, rows, PARTS, GROUP, CRO...  123 us

profile of v3, /device:TPU:0, one launch (start us, length us, event | category | flops | bytes accessed | tf_op | source)
XLA Modules:
  0.0 126.3 jit_solution(14946438428063654882)
XLA Ops:
  0.0 1.4 %fusion.weight_ref = f32[16,8,128]{2,1,0:T(8,128)} fusion(f32[8,128]{1,0:T(8,128)} %bitcast.8, s32[8,128]{1,0:T(8,128)} %bitcast.9), kind=kOutput, calls=%fused_computation | output fusion | flops 34823 | bytes 73728 | tf_op jit(solution)/shard_map/broadcast_in_dim | solution.py:363
  1.4 123.1 %shard_map.64 = bf16[128,2048]{1,0:T(8,128)(2,1)} custom-call(bf16[128,2048]{1,0:T(8,128)(2,1)} %tok_ref.1, f32[16,8,128]{2,1,0:T(8,128)} %fusion.weight_ref, bf16[2048,768]{1,0:T(8,128)(2,1)} %bitcast.5, bf16[2048,768]{1,0:T(8,128)(2,1)} %bitcast.6, bf16[768,2048]{1,0:T(8,128)(2,1)} %bitcast.7), custom_call_target="tpu_custom_call" | custom-call | tf_op jit(solution)/shard_map/pallas_call | solution.py:370
  124.5 1.9 %copy.8 = bf16[128,2048]{1,0:T(8,128)(2,1)} copy(bf16[128,2048]{1,0:T(8,128)(2,1)} %shard_map.64) | data formatting | bytes 1048576
